TPU v7x, 256 devices: a whole 4x4x8 slice. The times are simulated.
256 devices in a mesh: dp: 16 (over x_hi, y, core), seq: 16 (over z, x_lo).
Axes of the slice: x: 4 (x_hi: 2, x_lo: 2; x = x_hi * 2 + x_lo), y: 4, z: 8, core: 2. Of those that a mesh axis runs over, the one named last changes fastest.
Arguments:
- layer_input: bfloat16 [16, 2048, 5120], P('dp', 'seq'), may hold values from -6 to 6
- query_states: bfloat16 [16, 2048, 2560], P('dp', 'seq'), may hold values from -24 to 24
- key_states: bfloat16 [16, 2048, 512], P('dp', 'seq'), may hold values from -6 to 6
- out_grad: bfloat16 [16, 2048, 2560], P('dp', 'seq'), may hold values from -12 to 12
- value_weight: bfloat16 [5120, 512], P('dp'), may hold values from -0.078125 to 0.078125
- segment_ids: int32 [16, 2048], P('dp'), may hold values from 0 to 31, as said below
- pair_split: int32 [16, 32], P('dp'), may hold values from 1 to 2047, as said below
Outputs:
- query_grad: bfloat16 [16, 2048, 2560], P('dp', 'seq')
- key_grad: bfloat16 [16, 2048, 512], P('dp', 'seq')
- input_grad: bfloat16 [16, 2048, 5120], P('dp', 'seq')
- weight_grad: float32 [5120, 512], P('dp', 'seq')
Inputs may be any that keep to these rules, and one draw needn't show every extreme that they name: `segment_ids`: each packed row holds 32 sentence pairs numbered 0 to 31 in order along the row; each pair has 16 to 112 positions, every row has a pair of exactly 112, and the pair lengths of a row can be matched two by two into sums of 128. pair_split[r, s] lies after the first position of pair s and at or before its last position; in every row the first pair's second sentence begins at position 1 and the last pair's at position 2047.
All inputs are finite; a program needn't handle non-finite values.
Results may differ from a plain program's by a relative error of at most 0.0057.
Values may be sent and summed in bfloat16 or wider, within the bound.
A program may use at most 128 MiB of HBM per device.

v0:
```python
import jax
import jax.numpy as jnp
from jax import lax
from jax.sharding import PartitionSpec as P

HD = 128


def with_halo(cells, sides, width):
    for axis, dim in sides:
        count = lax.axis_size(axis)
        ends = count - 1
        head = lax.slice_in_dim(cells, 0, width, axis=dim)
        tail = lax.slice_in_dim(cells, cells.shape[dim] - width, cells.shape[dim], axis=dim)
        cells = jnp.concatenate(
            [
                lax.ppermute(tail, axis, [(i, (i + 1) % count) for i in range(ends)]),
                cells,
                lax.ppermute(head, axis, [((i + 1) % count, i) for i in range(ends)]),
            ],
            axis=dim,
        )
    return cells


def passed_along(array, axis, by):
    count = lax.axis_size(axis)
    pairs = [(i, i + by) for i in range(count) if 0 <= i + by < count]
    return lax.ppermute(array, axis, pairs)


def attend_block(query_rows, key_rows, value_rows, grad_rows, visible):
    rows_here = query_rows.shape[0]
    keys_here = key_rows.shape[0]
    head_count = key_rows.shape[1] // HD
    group_size = query_rows.shape[1] // key_rows.shape[1]
    score_scale = HD ** (-0.5)
    high = lax.Precision.HIGHEST
    query_split = query_rows.reshape(rows_here, head_count, group_size, HD)
    grad_split = grad_rows.reshape(rows_here, head_count, group_size, HD)
    key_split = key_rows.reshape(keys_here, head_count, HD)
    value_split = value_rows.reshape(keys_here, head_count, HD)
    query_parts = []
    key_parts = []
    value_parts = []
    for kv_group in range(head_count):
        query_head = query_split[:, kv_group]
        grad_head = grad_split[:, kv_group]
        key_head = key_split[:, kv_group]
        value_head = value_split[:, kv_group]
        scores = (
            jnp.einsum("qgd,kd->gqk", query_head, key_head, preferred_element_type=jnp.float32)
            * score_scale
        )
        masked = jnp.where(visible[None], scores, -1e30)
        highest = jnp.max(masked, axis=-1, keepdims=True)
        weights = jnp.where(visible[None], jnp.exp(masked - highest), 0.0)
        attention = weights / jnp.sum(weights, axis=-1, keepdims=True)
        attention_low = attention.astype(jnp.bfloat16)
        prob_grad = jnp.einsum(
            "qgd,kd->gqk", grad_head, value_head, preferred_element_type=jnp.float32
        )
        row_delta = jnp.sum(attention * prob_grad, axis=-1, keepdims=True)
        score_grad = attention * (prob_grad - row_delta)
        key_wide = key_head.astype(jnp.float32)
        query_wide = query_head.astype(jnp.float32)
        query_parts.append(
            jnp.einsum("gqk,kd->qgd", score_grad, key_wide, precision=high) * score_scale
        )
        key_parts.append(
            jnp.einsum("gqk,qgd->kd", score_grad, query_wide, precision=high) * score_scale
        )
        value_parts.append(
            jnp.einsum("gqk,qgd->kd", attention_low, grad_head, preferred_element_type=jnp.float32)
        )
    query_grad = jnp.stack(query_parts, axis=1).reshape(rows_here, -1)
    kv_grad = jnp.concatenate(key_parts + value_parts, axis=1)
    return (query_grad, kv_grad)


def local(layer_input, query_states, key_states, out_grad, value_weight, segment_ids, pair_split):
    layer_rows = layer_input[0]
    tok_count = layer_rows.shape[0]
    kv_width = key_states.shape[2]
    row_base = lax.axis_index("seq") * tok_count
    columns = layer_rows
    value_rows = jnp.dot(
        columns,
        lax.all_gather(value_weight, "dp", axis=0, tiled=True),
        preferred_element_type=jnp.float32,
    )
    value_low = value_rows.astype(jnp.bfloat16)
    both_states = jnp.concatenate([key_states[0], value_low], axis=1)
    extended = with_halo(both_states, (("seq", 0),), tok_count)
    key_block = extended[:, :kv_width]
    value_block = extended[:, kv_width:]
    seg_row = segment_ids[0]
    fill_ids = jnp.full((tok_count,), -1, jnp.int32)
    padded_ids = jnp.concatenate([fill_ids, seg_row, fill_ids])
    seg_key = lax.dynamic_slice_in_dim(padded_ids, row_base, tok_count + 2 * tok_count, 0)
    seg_query = lax.dynamic_slice_in_dim(seg_row, row_base, tok_count, 0)
    pair_numbers = jnp.arange(pair_split.shape[1], dtype=jnp.int32)
    split_query = jnp.sum(
        jnp.where(seg_query[:, None] == pair_numbers[None, :], pair_split[0][None, :], 0), axis=1
    )
    pos_query = row_base + jnp.arange(tok_count, dtype=jnp.int32)
    pos_key = row_base - tok_count + jnp.arange(tok_count + 2 * tok_count, dtype=jnp.int32)
    visible = (seg_key[None, :] == seg_query[:, None]) & (
        (pos_key[None, :] <= pos_query[:, None]) | (pos_key[None, :] < split_query[:, None])
    )
    query_grad, kv_grad = attend_block(
        query_states[0], key_block, value_block, out_grad[0], visible
    )
    lower_rim = kv_grad[:tok_count]
    upper_rim = kv_grad[tok_count + tok_count :]
    center = kv_grad[tok_count : tok_count + tok_count]
    from_upper = passed_along(lower_rim, "seq", -1)
    from_lower = passed_along(upper_rim, "seq", 1)
    center = center + from_upper + from_lower
    key_grad = center[:, :kv_width].astype(jnp.bfloat16)
    value_grad = center[:, kv_width:].astype(jnp.bfloat16)
    input_grad = lax.dot_general(
        value_grad,
        lax.all_gather(value_weight, "dp", axis=0, tiled=True),
        (((1,), (1,)), ((), ())),
        preferred_element_type=jnp.float32,
    )
    dp_count = lax.axis_size("dp")
    model_width = layer_rows.shape[1]
    input_blocks = lax.all_to_all(
        layer_rows.reshape(tok_count, dp_count, model_width // dp_count).transpose(1, 0, 2),
        "dp",
        0,
        0,
        tiled=True,
    )
    grad_rows = lax.all_gather(value_grad, "dp", axis=0, tiled=False)
    own_rows = jnp.einsum(
        "rtk,rtc->kc", input_blocks, grad_rows, preferred_element_type=jnp.float32
    )
    summed = lax.psum_scatter(own_rows, "seq", scatter_dimension=1, tiled=True)
    devices_all = lax.axis_size("dp") * lax.axis_size("seq")
    weight_grad = summed / devices_all
    return (
        query_grad.astype(jnp.bfloat16)[None],
        key_grad[None],
        input_grad.astype(jnp.bfloat16)[None],
        weight_grad,
    )


def solution(mesh):
    return jax.shard_map(
        local,
        mesh=mesh,
        in_specs=(
            P("dp", "seq", None),
            P("dp", "seq", None),
            P("dp", "seq", None),
            P("dp", "seq", None),
            P("dp", None),
            P("dp", None),
            P("dp", None),
        ),
        out_specs=(
            P("dp", "seq", None),
            P("dp", "seq", None),
            P("dp", "seq", None),
            P("dp", "seq"),
        ),
        check_vma=False,
    )
```

profile of v0, /device:TPU:8, one launch (start us, length us, event | category | flops | bytes accessed | tf_op | source)
XLA Modules:
  0.0 293.2 jit_solution(11749638976114022956)
XLA Ops:
  10.1 67.0 %all-gather.4.cloned.1.call-done = bf16[5120,512]{1,0:T(8,128)(2,1)} async-done(((bf16[320,512]{1,0:T(8,128)(2,1)}), bf16[5120,512]{1,0:T(8,128)(2,1)}) %all-gather.4.cloned.1.call-update) | async-done | bytes 5242896 | tf_op jit(solution)/shard_map/all_gather | solution.py:89
  77.2 3.7 %fusion.35 = bf16[128,512]{1,0:T(8,128)(2,1)S(1)} fusion(bf16[5120,512]{1,0:T(8,128)(2,1)} %all-gather.4.cloned.1.call-done, bf16[1,128,5120]{2,1,0:T(8,128)(2,1)} %param.7), kind=kOutput, calls=%fused_computation.53 | convolution fusion | flops 671154176 | bytes 6684672 | tf_op jit(solution)/shard_map/dot_general | solution.py:87
  82.4 5.3 %collective-permute-start = (bf16[128,1024]{1,0:T(8,128)(2,1)S(1)}, bf16[128,1024]{1,0:T(8,128)(2,1)}, u32[]{:S(2)}, u32[]{:S(2)}) collective-permute-start(bf16[128,1024]{1,0:T(8,128)(2,1)S(1)} %pad_maximum_fusion.2), channel_id=1, source_target_pairs={{0,1},{1,2},{2,3},{3,4},{4,5},{5,6},{6,7},{7,8},{8,9},{9,10},{10,1... | collective-permute-start | bytes 786440 | tf_op jit(solution)/shard_map/ppermute | solution.py:17
  88.6 2.9 collective-permute-done.1
  91.5 4.6 %collective-permute-done = bf16[128,1024]{1,0:T(8,128)(2,1)} collective-permute-done((bf16[128,1024]{1,0:T(8,128)(2,1)S(1)}, bf16[128,1024]{1,0:T(8,128)(2,1)}, u32[]{:S(2)}, u32[]{:S(2)}) %collective-permute-start) | collective-permute-done | bytes 262176 | tf_op jit(solution)/shard_map/ppermute | solution.py:17
  99.4 1.5 fusion.79
  102.3 1.4 fusion.77
  103.7 1.5 fusion.76
  105.3 1.6 multiply_reduce_fusion.3
  114.7 1.7 fusion.34
  116.4 1.7 fusion.33
  118.1 1.6 fusion.32
  119.7 1.6 fusion.31
  122.9 5.1 %collective-permute-start.3 = (f32[128,1024]{0,1:T(8,128)S(1)}, f32[128,1024]{0,1:T(8,128)S(1)}, u32[]{:S(2)}, u32[]{:S(2)}) collective-permute-start(f32[128,1024]{0,1:T(8,128)S(1)} %get-tuple-element.21), channel_id=1, source_target_pairs={{0,1},{1,2},{2,3},{3,4},{4,5},{5,6},{6,7},{7,8},{8,9},{9,10},{10,1... | collective-permute-start | bytes 1572872 | tf_op jit(solution)/shard_map/ppermute | solution.py:29
  128.0 10.1 %collective-permute-done.2 = f32[128,1024]{0,1:T(8,128)S(1)} collective-permute-done((f32[128,1024]{0,1:T(8,128)S(1)}, f32[128,1024]{0,1:T(8,128)S(1)}, u32[]{:S(2)}, u32[]{:S(2)}) %collective-permute-start.2) | collective-permute-done | bytes 524320 | tf_op jit(solution)/shard_map/ppermute | solution.py:29
  138.2 11.4 %collective-permute-done.3 = f32[128,1024]{0,1:T(8,128)S(1)} collective-permute-done((f32[128,1024]{0,1:T(8,128)S(1)}, f32[128,1024]{0,1:T(8,128)S(1)}, u32[]{:S(2)}, u32[]{:S(2)}) %collective-permute-start.3) | collective-permute-done | bytes 524320 | tf_op jit(solution)/shard_map/ppermute | solution.py:29
  150.3 1.4 copy.184
  151.8 6.2 %all-to-all-start = ((bf16[16,128,320]{1,2,0:T(8,128)(2,1)}), bf16[16,128,320]{1,2,0:T(8,128)(2,1)}, u32[]{:S(2)}, u32[]{:S(2)}) async-start(bf16[16,128,320]{1,2,0:T(8,128)(2,1)} %bitcast.64), calls=%async_computation | async-start | bytes 2621440 | tf_op jit(solution)/shard_map/all_to_all | solution.py:130
  158.1 50.0 %all-gather.6.cloned.1.call-done = bf16[2048,512]{0,1:T(8,128)(2,1)} async-done(((bf16[128,512]{0,1:T(8,128)(2,1)}), bf16[2048,512]{0,1:T(8,128)(2,1)}) %all-gather.6.cloned.1.call-update) | async-done | bytes 2097168 | tf_op jit(solution)/shard_map/all_gather | solution.py:137
  208.1 2.9 copy.217
  211.0 2.1 convolution_bitcast_fusion.4
  214.7 2.0 fusion.49
  222.4 5.4 %fusion.4 = bf16[1,128,5120]{2,1,0:T(8,128)(2,1)} fusion(bf16[5120,512]{1,0:T(8,128)(2,1)} %all-gather.4.cloned.1.call-done, bf16[128,1024]{0,1:T(8,128)(2,1)S(1)} %fusion.51), kind=kOutput, calls=%fused_computation.5 | convolution fusion | flops 671744000 | bytes 6684672 | tf_op jit(solution)/shard_map/dot_general | solution.py:122
  227.8 57.3 %reduce-scatter.4.cloned.1.call-done = f32[32,320]{1,0:T(8,128)} async-done(((f32[512,320]{1,0:T(8,128)}), f32[32,320]{1,0:T(8,128)}) %reduce-scatter.4.cloned.1.call-update) | async-done | bytes 40976
  (123 shorter events, 28.6 us)
Async XLA Ops:
  7.2 70.0 %all-gather.4.cloned.1.call-start = ((), (), s32[]{:S(2)}) async-start(), calls=%async_computation.2 | async-start | bytes 5570560 | tf_op jit(solution)/shard_map/all_gather | solution.py:89
  7.9 200.2 %all-gather.6.cloned.1.call-start = ((), (), s32[]{:S(2)}) async-start(), calls=%async_computation.3 | async-start | bytes 2228224 | tf_op jit(solution)/shard_map/all_gather | solution.py:137
  10.1 70.8 %copy-start.7 = (bf16[1,128,512]{2,1,0:T(8,128)(2,1)S(1)}, bf16[1,128,512]{2,1,0:T(8,128)(2,1)}, u32[]{:S(2)}) copy-start(bf16[1,128,512]{2,1,0:T(8,128)(2,1)} %param.9) | copy-start | bytes 393220
  10.1 77.6 %copy-start.1 = (bf16[1,128,2560]{2,1,0:T(8,128)(2,1)S(1)}, bf16[1,128,2560]{2,1,0:T(8,128)(2,1)}, u32[]{:S(2)}) copy-start(bf16[1,128,2560]{2,1,0:T(8,128)(2,1)} %param.8) | copy-start | bytes 1966084
  80.9 7.1 %copy-start.2 = (bf16[1,128,2560]{2,1,0:T(8,128)(2,1)S(1)}, bf16[1,128,2560]{2,1,0:T(8,128)(2,1)}, u32[]{:S(2)}) copy-start(bf16[1,128,2560]{2,1,0:T(8,128)(2,1)} %param.10) | copy-start | bytes 1966084
  81.0 10.5 %collective-permute-start.1 = (bf16[128,1024]{1,0:T(8,128)(2,1)S(1)}, bf16[128,1024]{1,0:T(8,128)(2,1)S(1)}, u32[]{:S(2)}, u32[]{:S(2)}) collective-permute-start(bf16[128,1024]{1,0:T(8,128)(2,1)S(1)} %pad_maximum_fusion.2), channel_id=1, source_target_pairs={{1,0},{2,1},{3,2},{4,3},{5,4},{6,5},{7,6},{8,7},{9,8},{10,9},{11,1... | collective-permute-start | bytes 786440 | tf_op jit(solution)/shard_map/ppermute | solution.py:19
  82.4 13.7 %collective-permute-start = (bf16[128,1024]{1,0:T(8,128)(2,1)S(1)}, bf16[128,1024]{1,0:T(8,128)(2,1)}, u32[]{:S(2)}, u32[]{:S(2)}) collective-permute-start(bf16[128,1024]{1,0:T(8,128)(2,1)S(1)} %pad_maximum_fusion.2), channel_id=1, source_target_pairs={{0,1},{1,2},{2,3},{3,4},{4,5},{5,6},{6,7},{7,8},{8,9},{9,10},{10,1... | collective-permute-start | bytes 786440 | tf_op jit(solution)/shard_map/ppermute | solution.py:17
  88.0 15.7 %copy-start.3 = (bf16[1,128,2560]{1,2,0:T(8,128)(2,1)}, bf16[1,128,2560]{1,2,0:T(8,128)(2,1)S(1)}, u32[]{:S(2)}) copy-start(bf16[1,128,2560]{1,2,0:T(8,128)(2,1)S(1)} %copy.143) | copy-start | bytes 1966084
  88.4 16.9 %copy-start.5 = (bf16[1,128,2560]{1,2,0:T(8,128)(2,1)}, bf16[1,128,2560]{1,2,0:T(8,128)(2,1)S(1)}, u32[]{:S(2)}) copy-start(bf16[1,128,2560]{1,2,0:T(8,128)(2,1)S(1)} %copy.146) | copy-start | bytes 1966084
  88.6 15.1 %copy-start.15 = (pred[128,384]{0,1:T(8,128)(4,1)}, pred[128,384]{0,1:T(8,128)(4,1)S(1)}, u32[]{:S(2)}) copy-start(pred[128,384]{0,1:T(8,128)(4,1)S(1)} %or_and_fusion) | copy-start | bytes 147460
  99.3 2.9 copy-start.8
  99.4 2.9 copy-start.10
  105.3 1.7 copy-start.22
  107.0 1.8 copy-start.20
  112.9 1.8 copy-start.37
  121.4 28.9 %copy-start = (bf16[1,128,5120]{2,1,0:T(8,128)(2,1)S(1)}, bf16[1,128,5120]{2,1,0:T(8,128)(2,1)}, u32[]{:S(2)}) copy-start(bf16[1,128,5120]{2,1,0:T(8,128)(2,1)} %param.7) | copy-start | bytes 3932164
  121.4 16.7 %collective-permute-start.2 = (f32[128,1024]{0,1:T(8,128)S(1)}, f32[128,1024]{0,1:T(8,128)S(1)}, u32[]{:S(2)}, u32[]{:S(2)}) collective-permute-start(f32[128,1024]{0,1:T(8,128)S(1)} %get-tuple-element.20), channel_id=1, source_target_pairs={{1,0},{2,1},{3,2},{4,3},{5,4},{6,5},{7,6},{8,7},{9,8},{10,9},{11,1... | collective-permute-start | bytes 1572872 | tf_op jit(solution)/shard_map/ppermute | solution.py:29
  122.9 26.7 %collective-permute-start.3 = (f32[128,1024]{0,1:T(8,128)S(1)}, f32[128,1024]{0,1:T(8,128)S(1)}, u32[]{:S(2)}, u32[]{:S(2)}) collective-permute-start(f32[128,1024]{0,1:T(8,128)S(1)} %get-tuple-element.21), channel_id=1, source_target_pairs={{0,1},{1,2},{2,3},{3,4},{4,5},{5,6},{6,7},{7,8},{8,9},{9,10},{10,1... | collective-permute-start | bytes 1572872 | tf_op jit(solution)/shard_map/ppermute | solution.py:29
  151.8 59.2 %all-to-all-start = ((bf16[16,128,320]{1,2,0:T(8,128)(2,1)}), bf16[16,128,320]{1,2,0:T(8,128)(2,1)}, u32[]{:S(2)}, u32[]{:S(2)}) async-start(bf16[16,128,320]{1,2,0:T(8,128)(2,1)} %bitcast.64), calls=%async_computation | async-start | bytes 2621440 | tf_op jit(solution)/shard_map/all_to_all | solution.py:130
  158.0 127.0 %reduce-scatter.4.cloned.1.call-start = ((), (), s32[]{:S(2)}) async-start(), calls=%async_computation.4 | async-start | bytes 835584
  214.7 2.1 copy-start.9
  214.7 2.1 copy-start.21
  214.7 2.1 copy-start.26
  214.7 2.1 copy-start.34
  (23 other events, 29.5 us)
Sparse Core Ops, SparseCore 0:
  10.8 66.3 all-gather.3
  150.5 57.6 all-gather.5
  214.5 70.4 reduce-scatter.3
where the time goes:
time: 294 us; the launch traced here: 293 us
  waiting for transfers between devices  204 us (69%)
  matrix products  33.3 us (11%)
  starting transfers between devices  19.6 us (7%)
  local copies, waits for them, and re-layouts  19 us (6%)
  between operations  14.3 us (5%)
    all_gather x1, waiting for transfers between devices, local(): lax.all_gather(value_weight, 'dp', axis=0, tiled=True)  67 us
    unnamed x4, waiting for transfers between devices  58 us
    all_gather x1, waiting for transfers between devices, local(): grad_rows = lax.all_gather(value_grad, 'dp', axis=0, tiled=False)  50 us
    ppermute x2, waiting for transfers between devices, passed_along(): return lax.ppermute(array, axis, pairs)  21.5 us
    unnamed x86, local copies, waits for them, and re-layouts  12.5 us
    dot_general x4, matrix products, attend_block(): jnp.einsum('gqk,qgd->kd', attention_low, grad_head, preferred_element_typ...  6.62 us
    ppermute x2, starting transfers between devices, passed_along(): return lax.ppermute(array, axis, pairs)  6.57 us
    all_to_all x1, starting transfers between devices, local(): lax.all_to_all(layer_rows.reshape(tok_count, dp_count, model_width // dp_...  6.25 us
  transfers between devices with their start and end apart: 8, of which 7 were waited for; matrix products, arithmetic and copies ran while one was open for 6% of the time, Pallas kernels for 0%

commit v1 on v0

--- a/solution.py
+++ b/solution.py
@@ -86,7 +86,9 @@
     columns = layer_rows
     value_rows = jnp.dot(
         columns,
-        lax.all_gather(value_weight, "dp", axis=0, tiled=True),
+        jnp.concatenate(
+            lax.all_to_all(jnp.stack([value_weight] * lax.axis_size("dp")), "dp", 0, 0), axis=0
+        ),
         preferred_element_type=jnp.float32,
     )
     value_low = value_rows.astype(jnp.bfloat16)

time: 294 us -> 380 us (1.29)
  waiting for transfers between devices: 204 us -> 273 us
  starting transfers between devices: 19.6 us -> 29.3 us
  local copies, waits for them, and re-layouts: 19 us -> 25.3 us
    all_to_all x0 -> x1, waiting for transfers between devices: none -> 75.7 us  [local(): lax.all_to_all(jnp.stack([value_weight] * lax.axis_size('dp')), 'dp', 0, 0)]
    all_gather x1, waiting for transfers between devices: 67 us -> 50.9 us  [local(): lax.all_gather(value_weight, 'dp', axis=0, tiled=True)]
    unnamed x4, waiting for transfers between devices: 58 us -> 68 us
    all_to_all x0 -> x1, starting transfers between devices: none -> 7.52 us  [local(): lax.all_to_all(jnp.stack([value_weight] * lax.axis_size('dp')), 'dp', 0, 0)]
    another operation x0 -> x1, local copies, waits for them, and re-layouts: none -> 3.85 us  [local(): jnp.stack([value_weight] * lax.axis_size('dp'))]
    unnamed x86 -> x96, local copies, waits for them, and re-layouts: 12.5 us -> 14.9 us
  transfers between devices with their start and end apart: 8 -> 9, of which waited for: 7 -> 7; matrix products, arithmetic and copies ran while one was open for 6% -> 6% of each run, Pallas kernels for 0% -> 0%
where the time goes in v1:
time: 380 us; the launch traced here: 379 us
  waiting for transfers between devices  273 us (72%)
  matrix products  33.1 us (9%)
  starting transfers between devices  29.3 us (8%)
  local copies, waits for them, and re-layouts  25.3 us (7%)
  between operations  14.3 us (4%)
  other arithmetic  4.13 us (1%)
    all_to_all x1, waiting for transfers between devices, local(): lax.all_to_all(jnp.stack([value_weight] * lax.axis_size('dp')), 'dp', 0, 0)  75.7 us
    unnamed x4, waiting for transfers between devices  68 us
    all_gather x1, waiting for transfers between devices, local(): grad_rows = lax.all_gather(value_grad, 'dp', axis=0, tiled=False)  52.2 us
    all_gather x1, waiting for transfers between devices, local(): lax.all_gather(value_weight, 'dp', axis=0, tiled=True)  50.9 us
    ppermute x2, waiting for transfers between devices, passed_along(): return lax.ppermute(array, axis, pairs)  21.3 us
    unnamed x96, local copies, waits for them, and re-layouts  14.9 us
    all_to_all x1, starting transfers between devices, local(): lax.all_to_all(layer_rows.reshape(tok_count, dp_count, model_width // dp_...  9.2 us
  transfers between devices with their start and end apart: 9, of which 7 were waited for; matrix products, arithmetic and copies ran while one was open for 6% of the time, Pallas kernels for 0%

profile of v1, /device:TPU:8, one launch (start us, length us, event | category | flops | bytes accessed | tf_op | source)
XLA Modules:
  0.0 379.1 jit_solution(13043934268772846819)
XLA Ops:
  7.2 3.8 %stack.17 = bf16[16,320,512]{2,1,0:T(8,128)(2,1)} broadcast(bf16[320,512]{1,0:T(8,128)(2,1)} %param.11), dimensions={1,2} | broadcast | bytes 5570560 | tf_op jit(solution)/shard_map/stack | solution.py:90
  11.0 7.5 %all-to-all-start = ((bf16[16,320,512]{2,1,0:T(8,128)(2,1)}), bf16[16,320,512]{2,1,0:T(8,128)(2,1)}, u32[]{:S(2)}, u32[]{:S(2)}) async-start(bf16[16,320,512]{2,1,0:T(8,128)(2,1)} %stack.17), calls=%async_computation | async-start | bytes 10485760 | tf_op jit(solution)/shard_map/all_to_all | solution.py:90
  18.8 75.7 %all-to-all-done = bf16[16,320,512]{2,1,0:T(8,128)(2,1)} async-done(((bf16[16,320,512]{2,1,0:T(8,128)(2,1)}), bf16[16,320,512]{2,1,0:T(8,128)(2,1)}, u32[]{:S(2)}, u32[]{:S(2)}) %all-to-all-start) | async-done | bytes 5242912 | tf_op jit(solution)/shard_map/all_to_all | solution.py:90
  94.6 3.4 fusion.35
  100.0 5.2 %collective-permute-start = (bf16[128,1024]{1,0:T(8,128)(2,1)}, bf16[128,1024]{1,0:T(8,128)(2,1)}, u32[]{:S(2)}, u32[]{:S(2)}) collective-permute-start(bf16[128,1024]{1,0:T(8,128)(2,1)} %pad_maximum_fusion.2), channel_id=1, source_target_pairs={{0,1},{1,2},{2,3},{3,4},{4,5},{5,6},{6,7},{7,8},{8,9},{9,10},{10,1... | collective-permute-start | bytes 786440 | tf_op jit(solution)/shard_map/ppermute | solution.py:17
  107.2 1.4 or_and_fusion
  108.8 4.8 %collective-permute-done = bf16[128,1024]{1,0:T(8,128)(2,1)} collective-permute-done((bf16[128,1024]{1,0:T(8,128)(2,1)}, bf16[128,1024]{1,0:T(8,128)(2,1)}, u32[]{:S(2)}, u32[]{:S(2)}) %collective-permute-start) | collective-permute-done | bytes 262176 | tf_op jit(solution)/shard_map/ppermute | solution.py:17
  121.9 1.5 fusion.79
  123.4 1.6 multiply_reduce_fusion.3
  132.8 1.8 fusion.34
  134.6 1.8 fusion.33
  136.4 1.8 fusion.32
  138.2 1.8 fusion.31
  140.1 4.6 %collective-permute-start.3 = (f32[128,1024]{0,1:T(8,128)S(1)}, f32[128,1024]{0,1:T(8,128)S(1)}, u32[]{:S(2)}, u32[]{:S(2)}) collective-permute-start(f32[128,1024]{0,1:T(8,128)S(1)} %get-tuple-element.21), channel_id=1, source_target_pairs={{0,1},{1,2},{2,3},{3,4},{4,5},{5,6},{6,7},{7,8},{8,9},{9,10},{10,1... | collective-permute-start | bytes 1572872 | tf_op jit(solution)/shard_map/ppermute | solution.py:29
  146.0 21.3 %collective-permute-done.3 = f32[128,1024]{0,1:T(8,128)S(1)} collective-permute-done((f32[128,1024]{0,1:T(8,128)S(1)}, f32[128,1024]{0,1:T(8,128)S(1)}, u32[]{:S(2)}, u32[]{:S(2)}) %collective-permute-start.3) | collective-permute-done | bytes 524320 | tf_op jit(solution)/shard_map/ppermute | solution.py:29
  170.9 9.2 %all-to-all-start.1 = ((bf16[16,128,320]{1,2,0:T(8,128)(2,1)}), bf16[16,128,320]{1,2,0:T(8,128)(2,1)S(1)}, u32[]{:S(2)}, u32[]{:S(2)}) async-start(bf16[16,128,320]{1,2,0:T(8,128)(2,1)} %bitcast.65), calls=%async_computation.1 | async-start | bytes 2621440 | tf_op jit(solution)/shard_map/all_to_all | solution.py:132
  180.2 52.2 %all-gather.6.cloned.1.call-done = bf16[2048,512]{0,1:T(8,128)(2,1)} async-done(((bf16[128,512]{0,1:T(8,128)(2,1)}), bf16[2048,512]{0,1:T(8,128)(2,1)}) %all-gather.6.cloned.1.call-update) | async-done | bytes 2097168 | tf_op jit(solution)/shard_map/all_gather | solution.py:139
  232.4 2.9 copy.217
  235.3 1.7 convolution_bitcast_fusion.4
  237.0 2.3 copy.218
  239.4 2.0 fusion.46
  247.4 50.9 %all-gather.4.cloned.1.call-done = bf16[5120,512]{1,0:T(8,128)(2,1)} async-done(((bf16[320,512]{1,0:T(8,128)(2,1)}), bf16[5120,512]{1,0:T(8,128)(2,1)}) %all-gather.4.cloned.1.call-update) | async-done | bytes 5242896 | tf_op jit(solution)/shard_map/all_gather | solution.py:126
  298.3 5.4 %fusion.4 = bf16[1,128,5120]{2,1,0:T(8,128)(2,1)} fusion(bf16[5120,512]{1,0:T(8,128)(2,1)} %all-gather.4.cloned.1.call-done, bf16[128,1024]{0,1:T(8,128)(2,1)S(1)} %copy-done.2), kind=kOutput, calls=%fused_computation.5 | convolution fusion | flops 671744000 | bytes 6684672 | tf_op jit(solution)/shard_map/dot_general | solution.py:124
  303.6 67.3 %reduce-scatter.4.cloned.1.call-done = f32[32,320]{1,0:T(8,128)} async-done(((f32[512,320]{1,0:T(8,128)}), f32[32,320]{1,0:T(8,128)}) %reduce-scatter.4.cloned.1.call-update) | async-done | bytes 40976
  (136 shorter events, 32.7 us)
Async XLA Ops:
  11.0 7.6 %copy-start.19 = (s32[1,2048]{1,0:T(1,128)S(1)}, s32[1,2048]{1,0:T(1,128)}, u32[]{:S(2)}) copy-start(s32[1,2048]{1,0:T(1,128)} %param.12) | copy-start | bytes 24580
  11.0 7.7 %copy-start.20 = (s32[1,32]{1,0:T(1,128)S(1)}, s32[1,32]{1,0:T(1,128)}, u32[]{:S(2)}) copy-start(s32[1,32]{1,0:T(1,128)} %param.13) | copy-start | bytes 388
  11.0 83.5 %copy-start = (bf16[1,128,5120]{2,1,0:T(8,128)(2,1)S(1)}, bf16[1,128,5120]{2,1,0:T(8,128)(2,1)}, u32[]{:S(2)}) copy-start(bf16[1,128,5120]{2,1,0:T(8,128)(2,1)} %param.7) | copy-start | bytes 3932164
  11.0 83.5 %all-to-all-start = ((bf16[16,320,512]{2,1,0:T(8,128)(2,1)}), bf16[16,320,512]{2,1,0:T(8,128)(2,1)}, u32[]{:S(2)}, u32[]{:S(2)}) async-start(bf16[16,320,512]{2,1,0:T(8,128)(2,1)} %stack.17), calls=%async_computation | async-start | bytes 10485760 | tf_op jit(solution)/shard_map/all_to_all | solution.py:90
  18.5 213.9 %all-gather.6.cloned.1.call-start = ((), (), s32[]{:S(2)}) async-start(), calls=%async_computation.4 | async-start | bytes 2228224 | tf_op jit(solution)/shard_map/all_gather | solution.py:139
  94.6 3.4 copy-start.6
  94.6 11.2 %copy-start.3 = (bf16[1,128,2560]{2,1,0:T(8,128)(2,1)S(1)}, bf16[1,128,2560]{2,1,0:T(8,128)(2,1)}, u32[]{:S(2)}) copy-start(bf16[1,128,2560]{2,1,0:T(8,128)(2,1)} %param.8) | copy-start | bytes 1966084
  98.0 8.1 %copy-start.4 = (bf16[1,128,2560]{2,1,0:T(8,128)(2,1)S(1)}, bf16[1,128,2560]{2,1,0:T(8,128)(2,1)}, u32[]{:S(2)}) copy-start(bf16[1,128,2560]{2,1,0:T(8,128)(2,1)} %param.10) | copy-start | bytes 1966084
  98.7 10.1 %collective-permute-start.1 = (bf16[128,1024]{1,0:T(8,128)(2,1)}, bf16[128,1024]{1,0:T(8,128)(2,1)}, u32[]{:S(2)}, u32[]{:S(2)}) collective-permute-start(bf16[128,1024]{1,0:T(8,128)(2,1)} %pad_maximum_fusion.2), channel_id=1, source_target_pairs={{1,0},{2,1},{3,2},{4,3},{5,4},{6,5},{7,6},{8,7},{9,8},{10,9},{11,1... | collective-permute-start | bytes 786440 | tf_op jit(solution)/shard_map/ppermute | solution.py:19
  100.0 13.5 %collective-permute-start = (bf16[128,1024]{1,0:T(8,128)(2,1)}, bf16[128,1024]{1,0:T(8,128)(2,1)}, u32[]{:S(2)}, u32[]{:S(2)}) collective-permute-start(bf16[128,1024]{1,0:T(8,128)(2,1)} %pad_maximum_fusion.2), channel_id=1, source_target_pairs={{0,1},{1,2},{2,3},{3,4},{4,5},{5,6},{6,7},{7,8},{8,9},{9,10},{10,1... | collective-permute-start | bytes 786440 | tf_op jit(solution)/shard_map/ppermute | solution.py:17
  116.1 4.4 %copy-start.9 = (bf16[384,1,128]{2,1,0:T(2,128)(2,1)}, bf16[384,1,128]{2,1,0:T(2,128)(2,1)S(1)}, u32[]{:S(2)}) copy-start(bf16[384,1,128]{2,1,0:T(2,128)(2,1)S(1)} %get-tuple-element.26) | copy-start | bytes 294916
  116.1 5.8 %copy-start.7 = (bf16[384,1,128]{2,1,0:T(2,128)(2,1)}, bf16[384,1,128]{2,1,0:T(2,128)(2,1)S(1)}, u32[]{:S(2)}) copy-start(bf16[384,1,128]{2,1,0:T(2,128)(2,1)S(1)} %get-tuple-element.24) | copy-start | bytes 294916
  127.2 4.8 %copy-start.35 = (f32[5,128,384]{1,2,0:T(8,128)}, f32[5,128,384]{1,2,0:T(8,128)S(1)}, u32[]{:S(2)}) copy-start(f32[5,128,384]{1,2,0:T(8,128)S(1)} %get-tuple-element.37) | copy-start | bytes 2949124
  127.2 4.8 %copy-start.42 = (f32[5,128]{1,0:T(8,128)}, f32[5,128]{1,0:T(8,128)S(1)}, u32[]{:S(2)}) copy-start(f32[5,128]{1,0:T(8,128)S(1)} %get-tuple-element.36) | copy-start | bytes 7684
  128.7 2.5 copy-start.31
  128.7 2.5 copy-start.38
  140.1 27.2 %collective-permute-start.3 = (f32[128,1024]{0,1:T(8,128)S(1)}, f32[128,1024]{0,1:T(8,128)S(1)}, u32[]{:S(2)}, u32[]{:S(2)}) collective-permute-start(f32[128,1024]{0,1:T(8,128)S(1)} %get-tuple-element.21), channel_id=1, source_target_pairs={{0,1},{1,2},{2,3},{3,4},{4,5},{5,6},{6,7},{7,8},{8,9},{9,10},{10,1... | collective-permute-start | bytes 1572872 | tf_op jit(solution)/shard_map/ppermute | solution.py:29
  144.7 22.6 %collective-permute-start.2 = (f32[128,1024]{0,1:T(8,128)S(1)}, f32[128,1024]{0,1:T(8,128)S(1)}, u32[]{:S(2)}, u32[]{:S(2)}) collective-permute-start(f32[128,1024]{0,1:T(8,128)S(1)} %get-tuple-element.20), channel_id=1, source_target_pairs={{1,0},{2,1},{3,2},{4,3},{5,4},{6,5},{7,6},{8,7},{9,8},{10,9},{11,1... | collective-permute-start | bytes 1572872 | tf_op jit(solution)/shard_map/ppermute | solution.py:29
  168.8 129.5 %all-gather.4.cloned.1.call-start = ((), (), s32[]{:S(2)}) async-start(), calls=%async_computation.3 | async-start | bytes 5570560 | tf_op jit(solution)/shard_map/all_gather | solution.py:126
  170.9 64.4 %all-to-all-start.1 = ((bf16[16,128,320]{1,2,0:T(8,128)(2,1)}), bf16[16,128,320]{1,2,0:T(8,128)(2,1)S(1)}, u32[]{:S(2)}, u32[]{:S(2)}) async-start(bf16[16,128,320]{1,2,0:T(8,128)(2,1)} %bitcast.65), calls=%async_computation.1 | async-start | bytes 2621440 | tf_op jit(solution)/shard_map/all_to_all | solution.py:132
  180.1 190.8 %reduce-scatter.4.cloned.1.call-start = ((), (), s32[]{:S(2)}) async-start(), calls=%async_computation.5 | async-start | bytes 835584
  237.0 2.4 copy-start.28
  237.0 2.4 copy-start.43
  245.4 52.8 %copy-start.2 = (bf16[128,1024]{0,1:T(8,128)(2,1)S(1)}, bf16[128,1024]{0,1:T(8,128)(2,1)}, u32[]{:S(2)}) copy-start(bf16[128,1024]{0,1:T(8,128)(2,1)} %copy-done.1) | copy-start | bytes 786436
  (29 other events, 42.1 us)
Sparse Core Ops, SparseCore 0:
  168.9 63.5 all-gather.5
  235.2 63.0 all-gather.3
  300.8 70.1 reduce-scatter.3
